TPU v7x, 32 devices: a whole 2x2x4 slice. The times are simulated.
32 devices in a mesh: rows: 8 (over z, x), chan: 4 (over y, core).
Axes of the slice: x: 2, y: 2, z: 4, core: 2. Of those that a mesh axis runs over, the one named last changes fastest.
Arguments:
- frames: bfloat16 [9, 32, 480, 256], P(None, 'rows', 'chan'), may hold values from -450 to 450
- spatial_weight: bfloat16 [256, 2304], P('rows'), may hold values from -0.125 to 0.125
- temporal_weight: bfloat16 [256, 768], P('rows'), may hold values from -0.21875 to 0.21875
- down_weight: bfloat16 [256, 2304], P('rows'), may hold values from -0.125 to 0.125
- norm_gain: float32 [256], replicated, may hold values from 0.5 to 1.5
- norm_shift: float32 [256], replicated, may hold values from -3 to 3
- down_bias: float32 [256], replicated, may hold values from -3 to 3
Outputs:
- latent: bfloat16 [9, 16, 240, 256], P(None, 'rows', 'chan')
All inputs are finite; a program needn't handle non-finite values.
Results may differ from a plain program's by a relative error of at most 0.0053.
Values may be sent and summed in bfloat16 or wider, within the bound.
No kernel may reach another device: no remote copies, remote signals or barrier semaphores. Data moves between devices by JAX's collectives and lax.ppermute only.
A program may use at most 128 MiB of HBM per device.

v0:
```python
import jax
import jax.numpy as jnp
from jax import lax
from jax.sharding import PartitionSpec as P

GROUPS = 32
epsilon = 1e-06


def extended_2(cells, sides, width):
    for axis, dim in sides:
        count = lax.axis_size(axis)
        ends = count - 1
        head = lax.slice_in_dim(cells, 0, width, axis=dim)
        tail = lax.slice_in_dim(cells, cells.shape[dim] - width, cells.shape[dim], axis=dim)
        cells = jnp.concatenate(
            [
                lax.ppermute(tail, axis, [(i, (i + 1) % count) for i in range(ends)]),
                cells,
                lax.ppermute(head, axis, [((i + 1) % count, i) for i in range(ends)]),
            ],
            axis=dim,
        )
    return cells


def passed_along(block, axis, distance):
    devices = range(lax.axis_size(axis))
    route = [(i - distance, i) for i in devices if i - distance in devices]
    return lax.ppermute(block, axis, route)


def spatial_taps(padded, weight_rows, width_out):
    rows_out = padded.shape[1] - 2
    cols_out = padded.shape[2] - 2
    summed = None
    for tap_index in range(9):
        row_offset = tap_index // 3
        col_offset = tap_index % 3
        window = padded[
            :, row_offset : row_offset + rows_out, col_offset : col_offset + cols_out, :
        ]
        weight_panel = weight_rows[:, tap_index * width_out : (tap_index + 1) * width_out]
        product = jnp.einsum(
            "fijc,co->fijo", window, weight_panel, preferred_element_type=jnp.float32
        )
        summed = product if summed is None else summed + product
    return summed


def temporal_taps(values, weight_rows, width_out):
    frame_count = values.shape[0]
    summed = None
    for tap_index in range(3):
        lag_frames = 2 - tap_index
        if lag_frames > 0:
            delayed = jnp.concatenate(
                [jnp.repeat(values[:1], lag_frames, axis=0), values[: frame_count - lag_frames]],
                axis=0,
            )
        else:
            delayed = values
        weight_panel = weight_rows[:, tap_index * width_out : (tap_index + 1) * width_out]
        product = jnp.einsum(
            "fijc,co->fijo", delayed, weight_panel, preferred_element_type=jnp.float32
        )
        summed = product if summed is None else summed + product
    return summed


def down_taps(extended, weight_rows, width_out):
    rows_out = (extended.shape[1] - 1) // 2
    cols_out = (extended.shape[2] - 1) // 2
    summed = None
    for tap_index in range(9):
        row_offset = tap_index // 3
        col_offset = tap_index % 3
        window = extended[
            :,
            row_offset : row_offset + 2 * rows_out : 2,
            col_offset : col_offset + 2 * cols_out : 2,
            :,
        ]
        weight_panel = weight_rows[:, tap_index * width_out : (tap_index + 1) * width_out]
        product = jnp.einsum(
            "fijc,co->fijo", window, weight_panel, preferred_element_type=jnp.float32
        )
        summed = product if summed is None else summed + product
    return summed


def group_reduce(partial_sums):
    return lax.psum(partial_sums, ("rows", "chan"))


def place_groups(channel_sums, group_width):
    local_sums = channel_sums.reshape(-1, group_width).sum(axis=1)
    return local_sums


def channel_values(group_vector, group_width):
    return jnp.repeat(group_vector, group_width)


def per_device(
    frames, spatial_weight, temporal_weight, down_weight, norm_gain, norm_shift, down_bias
):
    full_spatial, full_temporal, full_down = (
        lax.all_gather(spatial_weight, "rows", axis=0, tiled=True),
        lax.all_gather(temporal_weight, "rows", axis=0, tiled=True),
        lax.all_gather(down_weight, "rows", axis=0, tiled=True),
    )
    channels = full_spatial.shape[0]
    group_width = channels // GROUPS
    frame_count = frames.shape[0]
    rows_dev = frames.shape[1]
    width_all = frames.shape[2] * lax.axis_size("chan")
    cell_count = float(frame_count * rows_dev * lax.axis_size("rows") * width_all * group_width)
    padded = extended_2(frames, (("rows", 1), ("chan", 2)), 1)
    first = spatial_taps(padded, full_spatial, channels).astype(jnp.bfloat16)
    hidden = temporal_taps(first, full_temporal, channels)
    channel_sums = jnp.sum(hidden, axis=(0, 1, 2))
    totals = group_reduce(place_groups(channel_sums, group_width)[None])
    means = totals[0] / cell_count
    chan_mean = channel_values(means, group_width)
    centered = hidden - chan_mean
    spread = group_reduce(
        place_groups(jnp.sum(centered * centered, axis=(0, 1, 2)), group_width)[None]
    )
    variance = spread[0] / cell_count
    chan_var = channel_values(variance, group_width)
    act = jax.nn.silu(centered * lax.rsqrt(chan_var + epsilon) * norm_gain + norm_shift).astype(
        jnp.bfloat16
    )
    below = passed_along(act[:, :1], "rows", -1)
    extended = jnp.concatenate([act, below], axis=1)
    beside = passed_along(extended[:, :, :1], "chan", -1)
    extended = jnp.concatenate([extended, beside], axis=2)
    latent = down_taps(extended, full_down, channels) + down_bias
    return latent.astype(jnp.bfloat16)


def solution(mesh):
    placed = (
        P(None, "rows", "chan", None),
        P("rows", None),
        P("rows", None),
        P("rows", None),
        P(),
        P(),
        P(),
    )
    return jax.shard_map(
        per_device,
        mesh=mesh,
        in_specs=placed,
        out_specs=P(None, "rows", "chan", None),
        check_vma=False,
    )
```

profile of v0, /device:TPU:3, one launch (start us, length us, event | category | flops | bytes accessed | tf_op | source)
XLA Modules:
  0.0 319.5 jit_solution(4577024968184721207)
XLA Ops:
  9.4 3.2 collective-permute-start
  12.6 2.9 collective-permute-start.1
  15.5 22.7 %collective-permute-done = bf16[9,1,120,256]{3,2,1,0:T(8,128)(2,1)} collective-permute-done((bf16[9,1,120,256]{3,2,1,0:T(8,128)(2,1)S(1)}, bf16[9,1,120,256]{3,2,1,0:T(8,128)(2,1)}, u32[]{:S(2)}, u32[]{:S(2)}) %collective-permute-start) | collective-permute-done | bytes 552992 | tf_op jit(solution)/shard_map/ppermute | solution.py:18
  42.3 4.6 %collective-permute-start.2 = (bf16[9,6,1,256]{3,2,1,0:T(2,128)(2,1)S(1)}, bf16[9,6,1,256]{3,2,1,0:T(2,128)(2,1)S(1)}, u32[]{:S(2)}, u32[]{:S(2)}) collective-permute-start(bf16[9,6,1,256]{3,2,1,0:T(2,128)(2,1)S(1)} %get-tuple-element.6), channel_id=1, source_target_pairs={{0,1},{1,2},{2,3},{4,5},{5,6},{6,7},{8,9},{9,10},{10,11},{12,13},{... | collective-permute-start | bytes 82952 | tf_op jit(solution)/shard_map/ppermute | solution.py:18
  46.9 25.9 %all_gather.10 = bf16[256,768]{1,0:T(8,128)(2,1)} all-gather(bf16[32,768]{1,0:T(8,128)(2,1)S(1)} %copy-done.12), channel_id=1, replica_groups=mesh['rows'=8,'chan'=4] {'rows'}, dimensions={0}, use_global_device_ids=true | all-gather | bytes 442368 | tf_op jit(solution)/shard_map/all_gather | solution.py:110
  72.8 5.5 %collective-permute-start.3 = (bf16[9,6,1,256]{3,2,1,0:T(2,128)(2,1)S(1)}, bf16[9,6,1,256]{3,2,1,0:T(2,128)(2,1)S(1)}, u32[]{:S(2)}, u32[]{:S(2)}) collective-permute-start(bf16[9,6,1,256]{3,2,1,0:T(2,128)(2,1)S(1)} %get-tuple-element.5), channel_id=1, source_target_pairs={{1,0},{2,1},{3,2},{5,4},{6,5},{7,6},{9,8},{10,9},{11,10},{13,12},{... | collective-permute-start | bytes 82952 | tf_op jit(solution)/shard_map/ppermute | solution.py:20
  78.4 3.8 %fusion.15 = f32[9,4,120,256]{3,2,1,0:T(8,128)} fusion(bf16[9,6,120,256]{3,2,1,0:T(8,128)(2,1)S(1)} %constant_dynamic-update-slice_fusion, bf16[9,6,1,256]{3,2,1,0:T(2,128)(2,1)S(1)} %collective-permute-done.2, bf16[256,2304]{1,0:T(8,128)(2,1)} %all-gather.3.cloned.1.call-done), kind=kOutput, calls=%fused_computation.29 | convolution fusion | flops 570654720 | bytes 7900160 | tf_op jit(solution)/shard_map/fijc,co->fijo/dot_general | solution.py:44
  87.8 2.9 fusion.9
  93.6 3.9 %fusion = f32[9,4,120,256]{3,2,1,0:T(8,128)} fusion(bf16[9,4,120,256]{3,2,1,0:T(8,128)(2,1)S(1)} %copy-done, bf16[9,1,120,256]{3,2,1,0:T(8,128)(2,1)} %collective-permute-done, bf16[256,2304]{1,0:T(8,128)(2,1)S(1)} %copy-done.11), kind=kOutput, calls=%fused_computation.15 | convolution fusion | flops 571760640 | bytes 7319552 | tf_op jit(solution)/shard_map/fijc,co->fijo/dot_general | solution.py:44
  99.3 2.9 fusion.50
  102.2 12.6 %add_convert_fusion = bf16[9,4,120,256]{3,2,1,0:T(8,128)(2,1)} fusion(f32[9,4,120,256]{3,2,1,0:T(8,128)S(1)} %fusion.4, f32[9,4,120,256]{3,2,1,0:T(8,128)} %fusion.22, f32[9,4,120,256]{3,2,1,0:T(8,128)} %fusion.9, f32[9,4,120,256]{3,2,1,0:T(8,128)} %fusion.50, f32[9,4,120,256]{3,2,1,0:T(8,128)} %fusion.15, f32[9,4,120,256]{3,2,1,0:T(8,128)} %fusion.12, ...), kind=kOutput, calls=%fused_computation.7 | convolution fusion | flops 580608000 | bytes 41105408 | tf_op jit(solution)/shard_map/fijc,co->fijo/dot_general | solution.py:44
  120.4 3.0 fusion.65
  123.7 38.6 %psum.14 = f32[1,32]{1,0:T(1,128)S(1)} all-reduce(f32[1,32]{1,0:T(1,128)S(1)} %bitcast.127), channel_id=1, replica_groups=mesh['rows'=8,'chan'=4] {'rows','chan'}, use_global_device_ids=true, to_apply=%region_2.0 | all-reduce | flops 32 | bytes 256 | tf_op jit(solution)/shard_map/psum | solution.py:93
  165.5 41.8 %psum.15 = f32[1,32]{1,0:T(1,128)S(1)} all-reduce(f32[1,32]{1,0:T(1,128)S(1)} %bitcast.126), channel_id=1, replica_groups=mesh['rows'=8,'chan'=4] {'rows','chan'}, use_global_device_ids=true, to_apply=%region_5.0 | all-reduce | flops 32 | bytes 256 | tf_op jit(solution)/shard_map/psum | solution.py:93
  207.5 3.6 %multiply_convert_fusion = bf16[9,4,120,256]{3,2,1,0:T(8,128)(2,1)S(1)} fusion(f32[9,4,120,256]{3,2,1,0:T(8,128)} %get-tuple-element.12, f32[256]{0:T(256)S(1)} %copy-done.13, f32[256]{0:T(256)S(1)} %copy-done.14, f32[256]{0:T(256)S(1)} %rsqrt.16, f32[256]{0:T(256)S(1)} %sub.10), kind=kLoop, calls=%fused_computation.4 | loop fusion | flops 9953280 | bytes 6639616 | tf_op jit(solution)/shard_map/convert_element_type | solution.py:132
  217.1 10.4 %collective-permute-done.4 = bf16[9,1,120,256]{3,2,1,0:T(8,128)(2,1)S(1)} collective-permute-done((bf16[9,1,120,256]{3,2,1,0:T(8,128)(2,1)}, bf16[9,1,120,256]{3,2,1,0:T(8,128)(2,1)S(1)}, u32[]{:S(2)}, u32[]{:S(2)}) %collective-permute-start.4) | collective-permute-done | bytes 552992 | tf_op jit(solution)/shard_map/ppermute | solution.py:30
  229.3 10.3 %slice.188 = bf16[9,2,60,256]{3,2,1,0:T(8,128)(2,1)} slice(bf16[9,5,120,256]{3,2,1,0:T(8,128)(2,1)} %pad_maximum_fusion), slice={[0:9:1], [1:5:2], [0:120:2], [0:256:1]} | slice | bytes 1105920 | tf_op jit(solution)/shard_map/slice | solution.py:78
  239.6 8.5 %slice.194 = bf16[9,2,60,256]{3,2,1,0:T(8,128)(2,1)S(1)} slice(bf16[9,5,120,256]{3,2,1,0:T(8,128)(2,1)} %pad_maximum_fusion), slice={[0:9:1], [2:5:2], [0:120:2], [0:256:1]} | slice | bytes 1105920 | tf_op jit(solution)/shard_map/slice | solution.py:78
  248.2 4.5 %collective-permute-start.5 = (bf16[9,5,1,256]{3,2,1,0:T(2,128)(2,1)S(1)}, bf16[9,5,1,256]{3,2,1,0:T(2,128)(2,1)S(1)}, u32[]{:S(2)}, u32[]{:S(2)}) collective-permute-start(bf16[9,5,1,256]{3,2,1,0:T(2,128)(2,1)S(1)} %fusion.51), channel_id=1, source_target_pairs={{1,0},{2,1},{3,2},{5,4},{6,5},{7,6},{9,8},{10,9},{11,10},{13,12},{... | collective-permute-start | bytes 69128 | tf_op jit(solution)/shard_map/ppermute | solution.py:30
  259.2 10.5 %slice.184 = bf16[9,2,60,256]{3,2,1,0:T(8,128)(2,1)} slice(bf16[9,5,121,256]{3,2,1,0:T(8,128)(2,1)} %pad_maximum_fusion.1), slice={[0:9:1], [0:4:2], [1:121:2], [0:256:1]} | slice | bytes 1105920 | tf_op jit(solution)/shard_map/slice | solution.py:78
  269.6 10.2 %slice.198 = bf16[9,2,60,256]{3,2,1,0:T(8,128)(2,1)} slice(bf16[9,5,121,256]{3,2,1,0:T(8,128)(2,1)} %pad_maximum_fusion.1), slice={[0:9:1], [2:5:2], [2:121:2], [0:256:1]} | slice | bytes 1105920 | tf_op jit(solution)/shard_map/slice | solution.py:78
  279.8 10.1 %slice.196 = bf16[9,2,60,256]{3,2,1,0:T(8,128)(2,1)} slice(bf16[9,5,121,256]{3,2,1,0:T(8,128)(2,1)} %pad_maximum_fusion.1), slice={[0:9:1], [2:5:2], [1:121:2], [0:256:1]} | slice | bytes 1105920 | tf_op jit(solution)/shard_map/slice | solution.py:78
  289.9 6.0 %slice.192 = bf16[9,2,60,256]{3,2,1,0:T(8,128)(2,1)} slice(bf16[9,5,121,256]{3,2,1,0:T(8,128)(2,1)S(1)} %copy-done.2), slice={[0:9:1], [1:5:2], [2:121:2], [0:256:1]} | slice | bytes 1105920 | tf_op jit(solution)/shard_map/slice | solution.py:78
  295.9 5.9 %slice.190 = bf16[9,2,60,256]{3,2,1,0:T(8,128)(2,1)} slice(bf16[9,5,121,256]{3,2,1,0:T(8,128)(2,1)S(1)} %copy-done.2), slice={[0:9:1], [1:5:2], [1:121:2], [0:256:1]} | slice | bytes 1105920 | tf_op jit(solution)/shard_map/slice | solution.py:78
  (87 shorter events, 51.4 us)
Async XLA Ops:
  6.5 71.8 %all-gather.3.cloned.1.call-start = ((), (), s32[]{:S(2)}) async-start(), calls=%async_computation | async-start | bytes 1327104 | tf_op jit(solution)/shard_map/all_gather | solution.py:109
  7.3 207.6 %all-gather.5.cloned.1.call-start = ((), (), s32[]{:S(2)}) async-start(), calls=%async_computation.1 | async-start | bytes 1327104 | tf_op jit(solution)/shard_map/all_gather | solution.py:111
  9.4 28.8 %collective-permute-start = (bf16[9,1,120,256]{3,2,1,0:T(8,128)(2,1)S(1)}, bf16[9,1,120,256]{3,2,1,0:T(8,128)(2,1)}, u32[]{:S(2)}, u32[]{:S(2)}) collective-permute-start(bf16[9,1,120,256]{3,2,1,0:T(8,128)(2,1)S(1)} %get-tuple-element.9), channel_id=1, source_target_pairs={{0,4},{4,8},{8,12},{12,16},{16,20},{20,24},{24,28},{1,5},{5,9},{9,... | collective-permute-start | bytes 1658888 | tf_op jit(solution)/shard_map/ppermute | solution.py:18
  12.6 28.5 %collective-permute-start.1 = (bf16[9,1,120,256]{3,2,1,0:T(8,128)(2,1)}, bf16[9,1,120,256]{3,2,1,0:T(8,128)(2,1)}, u32[]{:S(2)}, u32[]{:S(2)}) collective-permute-start(bf16[9,1,120,256]{3,2,1,0:T(8,128)(2,1)} %get-tuple-element.10), channel_id=1, source_target_pairs={{4,0},{8,4},{12,8},{16,12},{20,16},{24,20},{28,24},{5,1},{9,5},{13... | collective-permute-start | bytes 1658888 | tf_op jit(solution)/shard_map/ppermute | solution.py:20
  39.3 7.6 %copy-start.12 = (bf16[32,768]{1,0:T(8,128)(2,1)S(1)}, bf16[32,768]{1,0:T(8,128)(2,1)}, u32[]{:S(2)}) copy-start(bf16[32,768]{1,0:T(8,128)(2,1)} %param.9) | copy-start | bytes 147460
  42.3 36.0 %collective-permute-start.2 = (bf16[9,6,1,256]{3,2,1,0:T(2,128)(2,1)S(1)}, bf16[9,6,1,256]{3,2,1,0:T(2,128)(2,1)S(1)}, u32[]{:S(2)}, u32[]{:S(2)}) collective-permute-start(bf16[9,6,1,256]{3,2,1,0:T(2,128)(2,1)S(1)} %get-tuple-element.6), channel_id=1, source_target_pairs={{0,1},{1,2},{2,3},{4,5},{5,6},{6,7},{8,9},{9,10},{10,11},{12,13},{... | collective-permute-start | bytes 82952 | tf_op jit(solution)/shard_map/ppermute | solution.py:18
  72.8 12.3 %collective-permute-start.3 = (bf16[9,6,1,256]{3,2,1,0:T(2,128)(2,1)S(1)}, bf16[9,6,1,256]{3,2,1,0:T(2,128)(2,1)S(1)}, u32[]{:S(2)}, u32[]{:S(2)}) collective-permute-start(bf16[9,6,1,256]{3,2,1,0:T(2,128)(2,1)S(1)} %get-tuple-element.5), channel_id=1, source_target_pairs={{1,0},{2,1},{3,2},{5,4},{6,5},{7,6},{9,8},{10,9},{11,10},{13,12},{... | collective-permute-start | bytes 82952 | tf_op jit(solution)/shard_map/ppermute | solution.py:20
  78.4 3.8 %copy-start.11 = (bf16[256,2304]{1,0:T(8,128)(2,1)S(1)}, bf16[256,2304]{1,0:T(8,128)(2,1)}, u32[]{:S(2)}) copy-start(bf16[256,2304]{1,0:T(8,128)(2,1)} %all-gather.3.cloned.1.call-done) | copy-start | bytes 3538948
  90.8 2.9 copy-start
  114.8 1.6 copy-start.1
  118.9 1.5 slice-start.1
  123.5 84.1 %copy-start.13 = (f32[256]{0:T(256)S(1)}, f32[256]{0:T(256)}, u32[]{:S(2)}) copy-start(f32[256]{0:T(256)} %param.12) | copy-start | bytes 3076
  123.5 84.1 %copy-start.14 = (f32[256]{0:T(256)S(1)}, f32[256]{0:T(256)}, u32[]{:S(2)}) copy-start(f32[256]{0:T(256)} %param.11) | copy-start | bytes 3076
  212.0 15.5 %collective-permute-start.4 = (bf16[9,1,120,256]{3,2,1,0:T(8,128)(2,1)}, bf16[9,1,120,256]{3,2,1,0:T(8,128)(2,1)S(1)}, u32[]{:S(2)}, u32[]{:S(2)}) collective-permute-start(bf16[9,1,120,256]{3,2,1,0:T(8,128)(2,1)} %slice.226), channel_id=1, source_target_pairs={{4,0},{8,4},{12,8},{16,12},{20,16},{24,20},{28,24},{5,1},{9,5},{13... | collective-permute-start | bytes 1658888 | tf_op jit(solution)/shard_map/ppermute | solution.py:30
  248.1 4.6 %copy-start.8 = (bf16[9,2,60,256]{3,2,1,0:T(8,128)(2,1)S(1)}, bf16[9,2,60,256]{3,2,1,0:T(8,128)(2,1)}, u32[]{:S(2)}) copy-start(bf16[9,2,60,256]{3,2,1,0:T(8,128)(2,1)} %slice.188) | copy-start | bytes 1658884
  248.2 9.0 %collective-permute-start.5 = (bf16[9,5,1,256]{3,2,1,0:T(2,128)(2,1)S(1)}, bf16[9,5,1,256]{3,2,1,0:T(2,128)(2,1)S(1)}, u32[]{:S(2)}, u32[]{:S(2)}) collective-permute-start(bf16[9,5,1,256]{3,2,1,0:T(2,128)(2,1)S(1)} %fusion.51), channel_id=1, source_target_pairs={{1,0},{2,1},{3,2},{5,4},{6,5},{7,6},{9,8},{10,9},{11,10},{13,12},{... | collective-permute-start | bytes 69128 | tf_op jit(solution)/shard_map/ppermute | solution.py:30
  259.2 30.7 %copy-start.2 = (bf16[9,5,121,256]{3,2,1,0:T(8,128)(2,1)S(1)}, bf16[9,5,121,256]{3,2,1,0:T(8,128)(2,1)}, u32[]{:S(2)}) copy-start(bf16[9,5,121,256]{3,2,1,0:T(8,128)(2,1)} %pad_maximum_fusion.1) | copy-start | bytes 8363524
  302.8 3.1 copy-start.9
  302.8 4.3 %copy-start.7 = (bf16[9,2,60,256]{3,2,1,0:T(8,128)(2,1)S(1)}, bf16[9,2,60,256]{3,2,1,0:T(8,128)(2,1)}, u32[]{:S(2)}) copy-start(bf16[9,2,60,256]{3,2,1,0:T(8,128)(2,1)} %slice.190) | copy-start | bytes 1658884
  304.3 4.2 %copy-start.5 = (f32[9,2,60,256]{3,2,1,0:T(8,128)S(1)}, f32[9,2,60,256]{3,2,1,0:T(8,128)}, u32[]{:S(2)}) copy-start(f32[9,2,60,256]{3,2,1,0:T(8,128)} %fusion.48) | copy-start | bytes 3317764
  304.3 4.2 %copy-start.6 = (bf16[9,2,60,256]{3,2,1,0:T(8,128)(2,1)S(1)}, bf16[9,2,60,256]{3,2,1,0:T(8,128)(2,1)}, u32[]{:S(2)}) copy-start(bf16[9,2,60,256]{3,2,1,0:T(8,128)(2,1)} %slice.184) | copy-start | bytes 1658884
  307.1 2.6 copy-start.3
  307.1 2.6 copy-start.4
  307.1 2.6 copy-start.15
  (2 other events, 2.5 us)
Sparse Core Ops, SparseCore 0:
  9.5 52.3 all-gather.2
  64.2 39.7 all-gather.4
where the time goes:
time: 322 us; the launch traced here: 320 us
  blocking collectives  106 us (33%)
  local copies, waits for them, and re-layouts  76.4 us (24%)
  matrix products  56 us (17%)
  waiting for transfers between devices  33.9 us (11%)
  starting transfers between devices  22.6 us (7%)
  between operations  13.8 us (4%)
  other arithmetic  10.5 us (3%)
    psum x2, blocking collectives, group_reduce(): return lax.psum(partial_sums, ('rows', 'chan'))  80.4 us
    slice x9, local copies, waits for them, and re-layouts, down_taps(): extended[:, row_offset:row_offset + 2 * rows_out:2, col_offset:col_offset...  63.3 us
    dot_general x9, matrix products, spatial_taps(): jnp.einsum('fijc,co->fijo', window, weight_panel, preferred_element_type=...  36.4 us
    all_gather x1, blocking collectives, per_device(): lax.all_gather(temporal_weight, 'rows', axis=0, tiled=True)  25.9 us
    ppermute x2, waiting for transfers between devices, extended_2(): lax.ppermute(tail, axis, [(i, (i + 1) % count) for i in range(ends)])  22.7 us
    dot_general x9, matrix products, down_taps(): jnp.einsum('fijc,co->fijo', window, weight_panel, preferred_element_type=...  15.1 us
    ppermute x2, waiting for transfers between devices, passed_along(): return lax.ppermute(block, axis, route)  10.4 us
    ppermute x2, starting transfers between devices, extended_2(): lax.ppermute(head, axis, [((i + 1) % count, i) for i in range(ends)])  8.43 us
  transfers between devices with their start and end apart: 8, of which 2 were waited for; matrix products, arithmetic and copies ran while one was open for 20% of the time, Pallas kernels for 0%

commit v1 on v0

--- a/solution.py
+++ b/solution.py
@@ -90,7 +90,7 @@
 
 
 def group_reduce(partial_sums):
-    return lax.psum(partial_sums, ("rows", "chan"))
+    return lax.psum(lax.psum(partial_sums, "chan"), "rows")
 
 
 def place_groups(channel_sums, group_width):

time: 322 us -> 289 us (0.90)
  blocking collectives: 106 us -> 74.2 us
    psum x2 -> x4, blocking collectives: 80.4 us -> 48.3 us  [group_reduce(): return lax.psum(lax.psum(partial_sums, 'chan'), 'rows')]
  transfers between devices with their start and end apart: 8 -> 8, of which waited for: 2 -> 2; matrix products, arithmetic and copies ran while one was open for 20% -> 22% of each run, Pallas kernels for 0% -> 0%
where the time goes in v1:
time: 289 us; the launch traced here: 287 us
  local copies, waits for them, and re-layouts  76.4 us (26%)
  blocking collectives  74.2 us (26%)
  matrix products  55.8 us (19%)
  waiting for transfers between devices  30.9 us (11%)
  starting transfers between devices  25.6 us (9%)
  between operations  13.8 us (5%)
  other arithmetic  10.5 us (4%)
    slice x9, local copies, waits for them, and re-layouts, down_taps(): extended[:, row_offset:row_offset + 2 * rows_out:2, col_offset:col_offset...  63.3 us
    psum x4, blocking collectives, group_reduce(): return lax.psum(lax.psum(partial_sums, 'chan'), 'rows')  48.3 us
    dot_general x9, matrix products, spatial_taps(): jnp.einsum('fijc,co->fijo', window, weight_panel, preferred_element_type=...  36.3 us
    all_gather x1, blocking collectives, per_device(): lax.all_gather(temporal_weight, 'rows', axis=0, tiled=True)  25.9 us
    ppermute x2, waiting for transfers between devices, extended_2(): lax.ppermute(tail, axis, [(i, (i + 1) % count) for i in range(ends)])  22.7 us
    dot_general x9, matrix products, down_taps(): jnp.einsum('fijc,co->fijo', window, weight_panel, preferred_element_type=...  15.1 us
    ppermute x2, starting transfers between devices, passed_along(): return lax.ppermute(block, axis, route)  9.41 us
    ppermute x2, starting transfers between devices, extended_2(): lax.ppermute(head, axis, [((i + 1) % count, i) for i in range(ends)])  8.43 us
  transfers between devices with their start and end apart: 8, of which 2 were waited for; matrix products, arithmetic and copies ran while one was open for 22% of the time, Pallas kernels for 0%

profile of v1, /device:TPU:3, one launch (start us, length us, event | category | flops | bytes accessed | tf_op | source)
XLA Modules:
  0.0 287.2 jit_solution(919798174334945147)
XLA Ops:
  9.4 3.2 %collective-permute-start = (bf16[9,1,120,256]{3,2,1,0:T(8,128)(2,1)S(1)}, bf16[9,1,120,256]{3,2,1,0:T(8,128)(2,1)}, u32[]{:S(2)}, u32[]{:S(2)}) collective-permute-start(bf16[9,1,120,256]{3,2,1,0:T(8,128)(2,1)S(1)} %get-tuple-element.9), channel_id=1, source_target_pairs={{0,4},{4,8},{8,12},{12,16},{16,20},{20,24},{24,28},{1,5},{5,9},{9,... | collective-permute-start | bytes 1658888 | tf_op jit(solution)/shard_map/ppermute | solution.py:18
  12.6 2.9 %collective-permute-start.1 = (bf16[9,1,120,256]{3,2,1,0:T(8,128)(2,1)}, bf16[9,1,120,256]{3,2,1,0:T(8,128)(2,1)}, u32[]{:S(2)}, u32[]{:S(2)}) collective-permute-start(bf16[9,1,120,256]{3,2,1,0:T(8,128)(2,1)} %get-tuple-element.10), channel_id=1, source_target_pairs={{4,0},{8,4},{12,8},{16,12},{20,16},{24,20},{28,24},{5,1},{9,5},{13... | collective-permute-start | bytes 1658888 | tf_op jit(solution)/shard_map/ppermute | solution.py:20
  15.5 22.7 %collective-permute-done = bf16[9,1,120,256]{3,2,1,0:T(8,128)(2,1)} collective-permute-done((bf16[9,1,120,256]{3,2,1,0:T(8,128)(2,1)S(1)}, bf16[9,1,120,256]{3,2,1,0:T(8,128)(2,1)}, u32[]{:S(2)}, u32[]{:S(2)}) %collective-permute-start) | collective-permute-done | bytes 552992 | tf_op jit(solution)/shard_map/ppermute | solution.py:18
  42.3 4.6 %collective-permute-start.2 = (bf16[9,6,1,256]{3,2,1,0:T(2,128)(2,1)S(1)}, bf16[9,6,1,256]{3,2,1,0:T(2,128)(2,1)S(1)}, u32[]{:S(2)}, u32[]{:S(2)}) collective-permute-start(bf16[9,6,1,256]{3,2,1,0:T(2,128)(2,1)S(1)} %get-tuple-element.6), channel_id=1, source_target_pairs={{0,1},{1,2},{2,3},{4,5},{5,6},{6,7},{8,9},{9,10},{10,11},{12,13},{... | collective-permute-start | bytes 82952 | tf_op jit(solution)/shard_map/ppermute | solution.py:18
  46.9 25.9 %all_gather.10 = bf16[256,768]{1,0:T(8,128)(2,1)} all-gather(bf16[32,768]{1,0:T(8,128)(2,1)S(1)} %copy-done.12), channel_id=1, replica_groups=mesh['rows'=8,'chan'=4] {'rows'}, dimensions={0}, use_global_device_ids=true | all-gather | bytes 442368 | tf_op jit(solution)/shard_map/all_gather | solution.py:110
  72.8 5.5 %collective-permute-start.3 = (bf16[9,6,1,256]{3,2,1,0:T(2,128)(2,1)S(1)}, bf16[9,6,1,256]{3,2,1,0:T(2,128)(2,1)S(1)}, u32[]{:S(2)}, u32[]{:S(2)}) collective-permute-start(bf16[9,6,1,256]{3,2,1,0:T(2,128)(2,1)S(1)} %get-tuple-element.5), channel_id=1, source_target_pairs={{1,0},{2,1},{3,2},{5,4},{6,5},{7,6},{9,8},{10,9},{11,10},{13,12},{... | collective-permute-start | bytes 82952 | tf_op jit(solution)/shard_map/ppermute | solution.py:20
  78.4 3.8 %fusion.15 = f32[9,4,120,256]{3,2,1,0:T(8,128)} fusion(bf16[9,6,120,256]{3,2,1,0:T(8,128)(2,1)S(1)} %constant_dynamic-update-slice_fusion, bf16[9,6,1,256]{3,2,1,0:T(2,128)(2,1)S(1)} %collective-permute-done.2, bf16[256,2304]{1,0:T(8,128)(2,1)} %all-gather.3.cloned.1.call-done), kind=kOutput, calls=%fused_computation.29 | convolution fusion | flops 570654720 | bytes 7900160 | tf_op jit(solution)/shard_map/fijc,co->fijo/dot_general | solution.py:44
  93.6 3.9 %fusion = f32[9,4,120,256]{3,2,1,0:T(8,128)} fusion(bf16[9,4,120,256]{3,2,1,0:T(8,128)(2,1)S(1)} %copy-done, bf16[9,1,120,256]{3,2,1,0:T(8,128)(2,1)} %collective-permute-done, bf16[256,2304]{1,0:T(8,128)(2,1)S(1)} %copy-done.11), kind=kOutput, calls=%fused_computation.15 | convolution fusion | flops 571760640 | bytes 7319552 | tf_op jit(solution)/shard_map/fijc,co->fijo/dot_general | solution.py:44
  102.1 12.6 %add_convert_fusion = bf16[9,4,120,256]{3,2,1,0:T(8,128)(2,1)} fusion(f32[9,4,120,256]{3,2,1,0:T(8,128)S(1)} %fusion.4, f32[9,4,120,256]{3,2,1,0:T(8,128)} %fusion.22, f32[9,4,120,256]{3,2,1,0:T(8,128)} %fusion.9, f32[9,4,120,256]{3,2,1,0:T(8,128)} %fusion.50, f32[9,4,120,256]{3,2,1,0:T(8,128)} %fusion.15, f32[9,4,120,256]{3,2,1,0:T(8,128)} %fusion.12, ...), kind=kOutput, calls=%fused_computation.7 | convolution fusion | flops 580608000 | bytes 41105408 | tf_op jit(solution)/shard_map/fijc,co->fijo/dot_general | solution.py:44
  120.3 3.0 %fusion.65 = (f32[256]{0:T(256)S(1)}, f32[9,4,120,256]{3,2,1,0:T(8,128)}) fusion(f32[9,4,120,256]{3,2,1,0:T(8,128)S(1)} %fusion.49, f32[9,4,120,256]{3,2,1,0:T(8,128)S(1)} %fusion.24, bf16[256,768]{1,0:T(8,128)(2,1)S(1)} %copy-done.10, bf16[8,4,120,256]{3,2,1,0:T(8,128)(2,1)S(1)} %slice-done.1, bf16[1,4,120,256]{3,2,1,0:T(8,128)(2,1)S(1)} %get-tuple-element.7), kind=kOutput, calls=%fused_computation.106 | convolution fusion | flops 570654464 | bytes 15614976 | tf_op jit(solution)/shard_map/fijc,co->fijo/dot_general | solution.py:64
  123.5 5.7 %psum.28 = f32[1,32]{1,0:T(1,128)S(1)} all-reduce(f32[1,32]{1,0:T(1,128)S(1)} %bitcast.127), channel_id=1, replica_groups=mesh['rows'=8,'chan'=4] {'chan'}, use_global_device_ids=true, to_apply=%region_2.0 | all-reduce | flops 32 | bytes 256 | tf_op jit(solution)/shard_map/psum | solution.py:93
  129.2 15.2 %psum.29 = f32[1,32]{1,0:T(1,128)S(1)} all-reduce(f32[1,32]{1,0:T(1,128)S(1)} %psum.28), channel_id=1, replica_groups=mesh['rows'=8,'chan'=4] {'rows'}, use_global_device_ids=true, to_apply=%region_3.0 | all-reduce | flops 32 | bytes 256 | tf_op jit(solution)/shard_map/psum | solution.py:93
  147.7 10.8 %psum.30 = f32[1,32]{1,0:T(1,128)S(1)} all-reduce(f32[1,32]{1,0:T(1,128)S(1)} %bitcast.126), channel_id=1, replica_groups=mesh['rows'=8,'chan'=4] {'chan'}, use_global_device_ids=true, to_apply=%region_6.0 | all-reduce | flops 32 | bytes 256 | tf_op jit(solution)/shard_map/psum | solution.py:93
  158.4 16.6 %psum.31 = f32[1,32]{1,0:T(1,128)S(1)} all-reduce(f32[1,32]{1,0:T(1,128)S(1)} %psum.30), channel_id=1, replica_groups=mesh['rows'=8,'chan'=4] {'rows'}, use_global_device_ids=true, to_apply=%region_7.0 | all-reduce | flops 32 | bytes 256 | tf_op jit(solution)/shard_map/psum | solution.py:93
  175.3 3.6 %multiply_convert_fusion = bf16[9,4,120,256]{3,2,1,0:T(8,128)(2,1)S(1)} fusion(f32[9,4,120,256]{3,2,1,0:T(8,128)} %get-tuple-element.12, f32[256]{0:T(256)S(1)} %copy-done.13, f32[256]{0:T(256)S(1)} %copy-done.14, f32[256]{0:T(256)S(1)} %rsqrt.16, f32[256]{0:T(256)S(1)} %sub.10), kind=kLoop, calls=%fused_computation.4 | loop fusion | flops 9953280 | bytes 6639616 | tf_op jit(solution)/shard_map/convert_element_type | solution.py:132
  184.8 7.4 %collective-permute-done.4 = bf16[9,1,120,256]{3,2,1,0:T(8,128)(2,1)S(1)} collective-permute-done((bf16[9,1,120,256]{3,2,1,0:T(8,128)(2,1)}, bf16[9,1,120,256]{3,2,1,0:T(8,128)(2,1)S(1)}, u32[]{:S(2)}, u32[]{:S(2)}) %collective-permute-start.4) | collective-permute-done | bytes 552992 | tf_op jit(solution)/shard_map/ppermute | solution.py:30
  194.0 10.3 %slice.188 = bf16[9,2,60,256]{3,2,1,0:T(8,128)(2,1)} slice(bf16[9,5,120,256]{3,2,1,0:T(8,128)(2,1)} %pad_maximum_fusion), slice={[0:9:1], [1:5:2], [0:120:2], [0:256:1]} | slice | bytes 1105920 | tf_op jit(solution)/shard_map/slice | solution.py:78
  204.3 8.5 %slice.194 = bf16[9,2,60,256]{3,2,1,0:T(8,128)(2,1)S(1)} slice(bf16[9,5,120,256]{3,2,1,0:T(8,128)(2,1)} %pad_maximum_fusion), slice={[0:9:1], [2:5:2], [0:120:2], [0:256:1]} | slice | bytes 1105920 | tf_op jit(solution)/shard_map/slice | solution.py:78
  212.9 7.5 %collective-permute-start.5 = (bf16[9,5,1,256]{3,2,1,0:T(2,128)(2,1)S(1)}, bf16[9,5,1,256]{3,2,1,0:T(2,128)(2,1)S(1)}, u32[]{:S(2)}, u32[]{:S(2)}) collective-permute-start(bf16[9,5,1,256]{3,2,1,0:T(2,128)(2,1)S(1)} %fusion.51), channel_id=1, source_target_pairs={{1,0},{2,1},{3,2},{5,4},{6,5},{7,6},{9,8},{10,9},{11,10},{13,12},{... | collective-permute-start | bytes 69128 | tf_op jit(solution)/shard_map/ppermute | solution.py:30
  226.9 10.5 %slice.184 = bf16[9,2,60,256]{3,2,1,0:T(8,128)(2,1)} slice(bf16[9,5,121,256]{3,2,1,0:T(8,128)(2,1)} %pad_maximum_fusion.1), slice={[0:9:1], [0:4:2], [1:121:2], [0:256:1]} | slice | bytes 1105920 | tf_op jit(solution)/shard_map/slice | solution.py:78
  237.4 10.1 %slice.198 = bf16[9,2,60,256]{3,2,1,0:T(8,128)(2,1)} slice(bf16[9,5,121,256]{3,2,1,0:T(8,128)(2,1)} %pad_maximum_fusion.1), slice={[0:9:1], [2:5:2], [2:121:2], [0:256:1]} | slice | bytes 1105920 | tf_op jit(solution)/shard_map/slice | solution.py:78
  247.5 10.1 %slice.196 = bf16[9,2,60,256]{3,2,1,0:T(8,128)(2,1)} slice(bf16[9,5,121,256]{3,2,1,0:T(8,128)(2,1)} %pad_maximum_fusion.1), slice={[0:9:1], [2:5:2], [1:121:2], [0:256:1]} | slice | bytes 1105920 | tf_op jit(solution)/shard_map/slice | solution.py:78
  257.6 6.0 %slice.192 = bf16[9,2,60,256]{3,2,1,0:T(8,128)(2,1)} slice(bf16[9,5,121,256]{3,2,1,0:T(8,128)(2,1)S(1)} %copy-done.2), slice={[0:9:1], [1:5:2], [2:121:2], [0:256:1]} | slice | bytes 1105920 | tf_op jit(solution)/shard_map/slice | solution.py:78
  263.6 5.9 %slice.190 = bf16[9,2,60,256]{3,2,1,0:T(8,128)(2,1)} slice(bf16[9,5,121,256]{3,2,1,0:T(8,128)(2,1)S(1)} %copy-done.2), slice={[0:9:1], [1:5:2], [1:121:2], [0:256:1]} | slice | bytes 1105920 | tf_op jit(solution)/shard_map/slice | solution.py:78
  (89 shorter events, 57.2 us)
Async XLA Ops:
  6.5 71.8 %all-gather.3.cloned.1.call-start = ((), (), s32[]{:S(2)}) async-start(), calls=%async_computation | async-start | bytes 1327104 | tf_op jit(solution)/shard_map/all_gather | solution.py:109
  7.3 175.3 %all-gather.5.cloned.1.call-start = ((), (), s32[]{:S(2)}) async-start(), calls=%async_computation.1 | async-start | bytes 1327104 | tf_op jit(solution)/shard_map/all_gather | solution.py:111
  9.4 28.8 %collective-permute-start = (bf16[9,1,120,256]{3,2,1,0:T(8,128)(2,1)S(1)}, bf16[9,1,120,256]{3,2,1,0:T(8,128)(2,1)}, u32[]{:S(2)}, u32[]{:S(2)}) collective-permute-start(bf16[9,1,120,256]{3,2,1,0:T(8,128)(2,1)S(1)} %get-tuple-element.9), channel_id=1, source_target_pairs={{0,4},{4,8},{8,12},{12,16},{16,20},{20,24},{24,28},{1,5},{5,9},{9,... | collective-permute-start | bytes 1658888 | tf_op jit(solution)/shard_map/ppermute | solution.py:18
  12.6 28.5 %collective-permute-start.1 = (bf16[9,1,120,256]{3,2,1,0:T(8,128)(2,1)}, bf16[9,1,120,256]{3,2,1,0:T(8,128)(2,1)}, u32[]{:S(2)}, u32[]{:S(2)}) collective-permute-start(bf16[9,1,120,256]{3,2,1,0:T(8,128)(2,1)} %get-tuple-element.10), channel_id=1, source_target_pairs={{4,0},{8,4},{12,8},{16,12},{20,16},{24,20},{28,24},{5,1},{9,5},{13... | collective-permute-start | bytes 1658888 | tf_op jit(solution)/shard_map/ppermute | solution.py:20
  39.3 7.6 %copy-start.12 = (bf16[32,768]{1,0:T(8,128)(2,1)S(1)}, bf16[32,768]{1,0:T(8,128)(2,1)}, u32[]{:S(2)}) copy-start(bf16[32,768]{1,0:T(8,128)(2,1)} %param.9) | copy-start | bytes 147460
  42.3 36.0 %collective-permute-start.2 = (bf16[9,6,1,256]{3,2,1,0:T(2,128)(2,1)S(1)}, bf16[9,6,1,256]{3,2,1,0:T(2,128)(2,1)S(1)}, u32[]{:S(2)}, u32[]{:S(2)}) collective-permute-start(bf16[9,6,1,256]{3,2,1,0:T(2,128)(2,1)S(1)} %get-tuple-element.6), channel_id=1, source_target_pairs={{0,1},{1,2},{2,3},{4,5},{5,6},{6,7},{8,9},{9,10},{10,11},{12,13},{... | collective-permute-start | bytes 82952 | tf_op jit(solution)/shard_map/ppermute | solution.py:18
  72.8 12.2 %collective-permute-start.3 = (bf16[9,6,1,256]{3,2,1,0:T(2,128)(2,1)S(1)}, bf16[9,6,1,256]{3,2,1,0:T(2,128)(2,1)S(1)}, u32[]{:S(2)}, u32[]{:S(2)}) collective-permute-start(bf16[9,6,1,256]{3,2,1,0:T(2,128)(2,1)S(1)} %get-tuple-element.5), channel_id=1, source_target_pairs={{1,0},{2,1},{3,2},{5,4},{6,5},{7,6},{9,8},{10,9},{11,10},{13,12},{... | collective-permute-start | bytes 82952 | tf_op jit(solution)/shard_map/ppermute | solution.py:20
  78.4 3.8 %copy-start.11 = (bf16[256,2304]{1,0:T(8,128)(2,1)S(1)}, bf16[256,2304]{1,0:T(8,128)(2,1)}, u32[]{:S(2)}) copy-start(bf16[256,2304]{1,0:T(8,128)(2,1)} %all-gather.3.cloned.1.call-done) | copy-start | bytes 3538948
  90.7 2.9 copy-start
  114.7 1.6 copy-start.1
  118.8 1.5 slice-start.1
  123.3 51.9 %copy-start.13 = (f32[256]{0:T(256)S(1)}, f32[256]{0:T(256)}, u32[]{:S(2)}) copy-start(f32[256]{0:T(256)} %param.12) | copy-start | bytes 3076
  123.3 51.9 %copy-start.14 = (f32[256]{0:T(256)S(1)}, f32[256]{0:T(256)}, u32[]{:S(2)}) copy-start(f32[256]{0:T(256)} %param.11) | copy-start | bytes 3076
  179.7 12.5 %collective-permute-start.4 = (bf16[9,1,120,256]{3,2,1,0:T(8,128)(2,1)}, bf16[9,1,120,256]{3,2,1,0:T(8,128)(2,1)S(1)}, u32[]{:S(2)}, u32[]{:S(2)}) collective-permute-start(bf16[9,1,120,256]{3,2,1,0:T(8,128)(2,1)} %slice.226), channel_id=1, source_target_pairs={{4,0},{8,4},{12,8},{16,12},{20,16},{24,20},{28,24},{5,1},{9,5},{13... | collective-permute-start | bytes 1658888 | tf_op jit(solution)/shard_map/ppermute | solution.py:30
  212.8 7.5 %copy-start.8 = (bf16[9,2,60,256]{3,2,1,0:T(8,128)(2,1)S(1)}, bf16[9,2,60,256]{3,2,1,0:T(8,128)(2,1)}, u32[]{:S(2)}) copy-start(bf16[9,2,60,256]{3,2,1,0:T(8,128)(2,1)} %slice.188) | copy-start | bytes 1658884
  212.9 12.0 %collective-permute-start.5 = (bf16[9,5,1,256]{3,2,1,0:T(2,128)(2,1)S(1)}, bf16[9,5,1,256]{3,2,1,0:T(2,128)(2,1)S(1)}, u32[]{:S(2)}, u32[]{:S(2)}) collective-permute-start(bf16[9,5,1,256]{3,2,1,0:T(2,128)(2,1)S(1)} %fusion.51), channel_id=1, source_target_pairs={{1,0},{2,1},{3,2},{5,4},{6,5},{7,6},{9,8},{10,9},{11,10},{13,12},{... | collective-permute-start | bytes 69128 | tf_op jit(solution)/shard_map/ppermute | solution.py:30
  226.9 30.7 %copy-start.2 = (bf16[9,5,121,256]{3,2,1,0:T(8,128)(2,1)S(1)}, bf16[9,5,121,256]{3,2,1,0:T(8,128)(2,1)}, u32[]{:S(2)}) copy-start(bf16[9,5,121,256]{3,2,1,0:T(8,128)(2,1)} %pad_maximum_fusion.1) | copy-start | bytes 8363524
  270.5 3.1 %copy-start.9 = (bf16[9,2,60,256]{3,2,1,0:T(8,128)(2,1)S(1)}, bf16[9,2,60,256]{3,2,1,0:T(8,128)(2,1)}, u32[]{:S(2)}) copy-start(bf16[9,2,60,256]{3,2,1,0:T(8,128)(2,1)} %slice.192) | copy-start | bytes 1658884
  270.5 4.3 %copy-start.7 = (bf16[9,2,60,256]{3,2,1,0:T(8,128)(2,1)S(1)}, bf16[9,2,60,256]{3,2,1,0:T(8,128)(2,1)}, u32[]{:S(2)}) copy-start(bf16[9,2,60,256]{3,2,1,0:T(8,128)(2,1)} %slice.190) | copy-start | bytes 1658884
  272.0 4.2 %copy-start.5 = (f32[9,2,60,256]{3,2,1,0:T(8,128)S(1)}, f32[9,2,60,256]{3,2,1,0:T(8,128)}, u32[]{:S(2)}) copy-start(f32[9,2,60,256]{3,2,1,0:T(8,128)} %fusion.48) | copy-start | bytes 3317764
  272.1 4.2 %copy-start.6 = (bf16[9,2,60,256]{3,2,1,0:T(8,128)(2,1)S(1)}, bf16[9,2,60,256]{3,2,1,0:T(8,128)(2,1)}, u32[]{:S(2)}) copy-start(bf16[9,2,60,256]{3,2,1,0:T(8,128)(2,1)} %slice.184) | copy-start | bytes 1658884
  274.8 2.6 copy-start.3
  274.8 2.6 copy-start.4
  274.8 2.6 copy-start.15
  (2 other events, 2.5 us)
Sparse Core Ops, SparseCore 0:
  9.5 52.3 all-gather.2
  64.2 39.7 all-gather.4
